TPU v7x, 32 devices: a whole 2x2x4 slice. The times are simulated.
32 devices in a mesh: lat: 2 (over y), lon: 8 (over z, x), lev: 2 (over core).
Axes of the slice: x: 2, y: 2, z: 4, core: 2. Of those that a mesh axis runs over, the one named last changes fastest.
Arguments:
- tokens: bfloat16 [4, 12, 96, 192], P('lev', 'lat', 'lon'), may hold values from -6 to 6
- norm1_gain: float32 [192], replicated, may hold values from 0.8 to 10
- qkv_weight: bfloat16 [192, 576], replicated, may hold values from -0.4375 to 0.4375
- proj_weight: bfloat16 [192, 192], replicated, may hold values from -0.4375 to 0.4375
- earth_bias: bfloat16 [2, 2, 6, 3312], P(None, 'lat'), may hold values from -4 to 4
- norm2_gain: float32 [192], replicated, may hold values from 0.5 to 1.5
- fc1_weight: bfloat16 [192, 768], replicated, may hold values from -0.4375 to 0.4375
- fc2_weight: bfloat16 [768, 192], replicated, may hold values from -0.21875 to 0.21875
Outputs:
- blended: bfloat16 [4, 12, 96, 192], P('lev', 'lat', 'lon')
All inputs are finite; a program needn't handle non-finite values.
Results may differ from a plain program's by a relative error of at most 0.008.
The roundings to bfloat16 on the way count: a program that leaves them out, or rounds other values in their place, can miss the bound.
Values may be sent and summed in bfloat16 or wider, within the bound.
A program may use at most 64 MiB of HBM per device.

v0:
```python
import jax
import jax.numpy as jnp
from jax import lax
from jax.sharding import PartitionSpec as P

HEADS = 6
WLV = 2
WLA = 6
WLO = 12


norm_eps = 1e-05


def padded(x, sides, width):
    for axis, dim in sides:
        size, length = (lax.axis_size(axis), x.shape[dim])
        up = [(i, (i + 1) % size) for i in range(size - 1)]
        down = [(j, i) for i, j in up]
        last = lax.slice_in_dim(x, length - width, length, axis=dim)
        first = lax.slice_in_dim(x, 0, width, axis=dim)
        before = lax.ppermute(last, axis, up)
        after = lax.ppermute(first, axis, down)
        x = jnp.concatenate([before, x, after], axis=dim)
    return x


def from_behind(block, axis, distance):
    devices = range(lax.axis_size(axis))
    route = [((i - distance) % len(devices), i) for i in devices]
    return lax.ppermute(block, axis, route)


def layer_norm(values, scale_gain):
    average = jnp.mean(values, axis=-1, keepdims=True)
    centered = values - average
    variance = jnp.mean(centered * centered, axis=-1, keepdims=True)
    return centered * lax.rsqrt(variance + norm_eps) * scale_gain


def window_coords():
    places = jnp.arange(WLV * WLA * WLO, dtype=jnp.int32)
    return (places // (WLA * WLO), places // WLO % WLA, places % WLO)


def bias_index():
    lev_place, lat_place, lon_place = window_coords()
    paired = (lev_place[:, None] * WLV + lev_place[None, :]) * WLA + lat_place[:, None]
    paired = paired * WLA + lat_place[None, :]
    return paired * (2 * WLO - 1) + lon_place[:, None] - lon_place[None, :] + WLO - 1


def region_of(places, extent, window):
    return jnp.where(
        places < extent - window, 0, jnp.where(places < extent - window // 2, 1, 2)
    ).astype(jnp.int32)


def attend_windows(windows, qkv_weight, bias_terms, allowed):
    lat_windows, lon_windows, window_size, feature_width = windows.shape
    head_dim = feature_width // HEADS
    projected = jnp.dot(
        windows.reshape(-1, feature_width), qkv_weight, preferred_element_type=jnp.float32
    )
    projected = projected.astype(jnp.bfloat16).reshape(
        lat_windows, lon_windows, window_size, 3, HEADS, head_dim
    )
    queries = projected[:, :, :, 0]
    key_rows = projected[:, :, :, 1]
    value_rows = projected[:, :, :, 2]
    scores = jnp.einsum("abqhd,abkhd->abhqk", queries, key_rows, preferred_element_type=jnp.float32)
    scores = scores * head_dim ** (-0.5) + bias_terms[:, None].astype(jnp.float32)
    scores = jnp.where(allowed[:, None, None], scores, -1e30)
    row_max = jnp.max(scores, axis=-1, keepdims=True)
    weights = jnp.exp(scores - row_max)
    probs = (weights / jnp.sum(weights, axis=-1, keepdims=True)).astype(jnp.bfloat16)
    context = jnp.einsum(
        "abhqk,abkhd->abqhd", probs, value_rows, preferred_element_type=jnp.float32
    )
    return context.astype(jnp.bfloat16).reshape(
        lat_windows, lon_windows, window_size, feature_width
    )


def rim_levlat(blocks):
    lev_cells, lat_cells, lon_cells, feature_width = blocks.shape
    grouped = blocks.reshape(lev_cells, lat_cells // (WLA // 2), WLA // 2, lon_cells, feature_width)
    widened = padded(grouped, (("lev", 0), ("lat", 1)), 1)
    return widened.reshape(lev_cells + WLV, lat_cells + WLA, lon_cells, feature_width)


def along_lon(blocks):
    ahead = from_behind(blocks[:, :, : WLO // 2], "lon", -1)
    widened = jnp.concatenate([blocks[:, :, WLO // 2 :], ahead], axis=2)
    return widened


def per_device(
    tokens, norm1_gain, qkv_weight, proj_weight, earth_bias, norm2_gain, fc1_weight, fc2_weight
):
    lev_cells, lat_cells, lon_cells, feature_width = tokens.shape
    half_lev, half_lat, half_lon = (WLV // 2, WLA // 2, WLO // 2)
    total_lev = lev_cells * lax.axis_size("lev")
    total_lat = lat_cells * lax.axis_size("lat")
    lev_start = lax.axis_index("lev") * lev_cells
    lat_start = lax.axis_index("lat") * lat_cells
    lev_types = total_lev // WLV
    window_size = WLV * WLA * WLO
    normed = layer_norm(tokens.astype(jnp.float32), norm1_gain).astype(jnp.bfloat16)
    extended = rim_levlat(along_lon(normed))
    edge_tables = from_behind(earth_bias, "lat", 1)
    all_tables = jnp.concatenate([edge_tables, earth_bias], axis=1)
    table_index = bias_index()
    lev_place, lat_place, lon_place = window_coords()
    lat_windows = (lat_cells + WLA) // WLA
    ext_columns = extended.shape[2]
    lon_windows = ext_columns // WLO
    lat_rolled = jnp.mod(
        lat_start
        - WLA
        + jnp.arange(lat_windows, dtype=jnp.int32)[:, None] * WLA
        + lat_place[None, :],
        total_lat,
    )
    lat_region = region_of(lat_rolled, total_lat, WLA)
    lat_allowed = lat_region[:, :, None] == lat_region[:, None, :]
    pieces = []
    for lev_window in range(lev_cells // WLV + 1):
        slab = extended[lev_window * WLV : (lev_window + 1) * WLV]
        windows = slab.reshape(WLV, lat_windows, WLA, lon_windows, WLO, feature_width).transpose(
            1, 3, 0, 2, 4, 5
        )
        windows = windows.reshape(lat_windows, lon_windows, window_size, feature_width)
        lev_type = jnp.mod(lev_start // WLV - 1 + lev_window, lev_types)
        lev_tables = jnp.take(all_tables, lev_type, axis=0)
        bias_terms = jnp.take(lev_tables, table_index, axis=2)
        lev_rolled = jnp.mod(lev_start - WLV + lev_window * WLV + lev_place, total_lev)
        lev_region = region_of(lev_rolled, total_lev, WLV)
        allowed = lat_allowed & (lev_region[:, None] == lev_region[None, :])[None]
        context = attend_windows(windows, qkv_weight, bias_terms, allowed)
        context = context.reshape(lat_windows, lon_windows, WLV, WLA, WLO, feature_width).transpose(
            2, 0, 3, 1, 4, 5
        )
        pieces.append(context.reshape(WLV, lat_windows * WLA, ext_columns, feature_width))
    inner = jnp.concatenate(pieces, axis=0)[
        half_lev : half_lev + lev_cells, half_lat : half_lat + lat_cells
    ]
    behind = from_behind(inner[:, :, -half_lon:], "lon", 1)
    context_own = jnp.concatenate([behind, inner[:, :, :-half_lon]], axis=2)
    first = tokens.reshape(-1, feature_width).astype(jnp.float32) + jnp.dot(
        context_own.reshape(-1, feature_width), proj_weight, preferred_element_type=jnp.float32
    )
    normed_two = layer_norm(first, norm2_gain).astype(jnp.bfloat16)
    hidden = jax.nn.gelu(
        jnp.dot(normed_two, fc1_weight, preferred_element_type=jnp.float32), approximate=False
    ).astype(jnp.bfloat16)
    result = first + jnp.dot(hidden, fc2_weight, preferred_element_type=jnp.float32)
    return result.astype(jnp.bfloat16).reshape(tokens.shape)


def solution(mesh):
    placed = (
        P("lev", "lat", "lon", None),
        P(),
        P(),
        P(),
        P(None, "lat", None, None),
        P(),
        P(),
        P(),
    )
    return jax.shard_map(
        per_device,
        mesh=mesh,
        in_specs=placed,
        out_specs=P("lev", "lat", "lon", None),
        check_vma=False,
    )
```

profile of v0, /device:TPU:0, one launch (start us, length us, event | category | flops | bytes accessed | tf_op | source)
XLA Modules:
  0.0 212.0 jit_solution(10097252631006876232)
XLA Ops:
  0.0 3.0 %collective-permute-start.5 = (bf16[2,1,6,3312]{3,0,2,1:T(2,128)(2,1)}, bf16[2,1,6,3312]{3,0,2,1:T(2,128)(2,1)S(1)}, u32[]{:S(2)}, u32[]{:S(2)}) collective-permute-start(bf16[2,1,6,3312]{3,0,2,1:T(2,128)(2,1)} %param.16), channel_id=1, source_target_pairs={{16,0},{0,16},{17,1},{1,17},{18,2},{2,18},{19,3},{3,19},{20,4},{4,... | collective-permute-start | bytes 238472 | tf_op jit(solution)/shard_map/ppermute | solution.py:31
  3.0 1.0 convert_reduce_fusion
  4.0 1.1 multiply_reduce_fusion
  5.1 1.0 multiply_convert_fusion
  6.1 4.6 %collective-permute-start = (bf16[2,6,6,192]{3,2,1,0:T(8,128)(2,1)S(1)}, bf16[2,6,6,192]{3,2,1,0:T(8,128)(2,1)S(1)}, u32[]{:S(2)}, u32[]{:S(2)}) collective-permute-start(bf16[2,6,6,192]{3,2,1,0:T(8,128)(2,1)S(1)} %get-tuple-element.32), channel_id=1, source_target_pairs={{2,0},{4,2},{6,4},{8,6},{10,8},{12,10},{14,12},{0,14},{3,1},{5,3},... | collective-permute-start | bytes 82952 | tf_op jit(solution)/shard_map/ppermute | solution.py:31
  11.3 0.8 compare_and_fusion.1
  12.6 1.3 collective-permute-start.1
  13.9 1.3 collective-permute-start.2
  15.4 1.6 collective-permute-done.2
  17.4 0.7 fusion.103
  18.1 3.0 %collective-permute-start.3 = (bf16[4,1,3,12,192]{4,0,3,2,1:T(4,128)(2,1)}, bf16[4,1,3,12,192]{4,0,3,2,1:T(4,128)(2,1)}, u32[]{:S(2)}, u32[]{:S(2)}) collective-permute-start(bf16[4,1,3,12,192]{4,0,3,2,1:T(4,128)(2,1)} %get-tuple-element.28), channel_id=1, source_target_pairs={{0,16},{1,17},{2,18},{3,19},{4,20},{5,21},{6,22},{7,23},{8,24},{9,... | collective-permute-start | bytes 165896 | tf_op jit(solution)/shard_map/ppermute | solution.py:22
  21.1 1.5 collective-permute-start.4
  22.7 0.4 broadcast_select_fusion.1
  23.2 2.4 %copy.82 = bf16[1,2,6,3312]{2,1,3,0:T(2,128)(2,1)S(1)} copy(bf16[1,2,6,3312]{3,0,2,1:T(2,128)(2,1)S(1)} %get-tuple-element.26) | data formatting | bytes 158976 | tf_op jit(solution)/shard_map/jit(_take)/select_n | solution.py:135
  25.5 51.4 %gather_fusion = bf16[20736,2,6]{2,1,0:T(2,128)(2,1)} fusion(bf16[2,6,3312]{1,0,2:T(2,128)(2,1)S(1)} %bitcast.108, s32[21504]{0:T(1024)S(1)} %pad_clamp_fusion), kind=kCustom, calls=%fused_computation.clone | custom fusion | bytes 1078272 | tf_op jit(solution)/shard_map/jit(_take)/gather | solution.py:136
  77.0 27.8 %copy.61 = bf16[144,144,2,6]{0,1,3,2:T(8,128)(2,1)S(1)} copy(bf16[144,144,2,6]{3,2,1,0:T(2,128)(2,1)} %bitcast.106) | data formatting | bytes 995328 | tf_op jit(solution)/shard_map/jit(_take)/gather | solution.py:136
  104.8 2.4 %copy.85 = bf16[1,2,6,3312]{2,1,3,0:T(2,128)(2,1)S(1)} copy(bf16[1,2,6,3312]{3,0,2,1:T(2,128)(2,1)S(1)} %get-tuple-element.27) | data formatting | bytes 158976 | tf_op jit(solution)/shard_map/jit(_take)/select_n | solution.py:135
  107.1 51.4 %gather_fusion.1 = bf16[20736,2,6]{2,1,0:T(2,128)(2,1)} fusion(bf16[2,6,3312]{1,0,2:T(2,128)(2,1)S(1)} %bitcast.107, s32[21504]{0:T(1024)S(1)} %pad_clamp_fusion), kind=kCustom, calls=%fused_computation.1.clone | custom fusion | bytes 1078272 | tf_op jit(solution)/shard_map/jit(_take)/gather | solution.py:136
  158.6 27.8 %copy.74 = bf16[144,144,2,6]{0,1,3,2:T(8,128)(2,1)S(1)} copy(bf16[144,144,2,6]{3,2,1,0:T(2,128)(2,1)} %bitcast.105) | data formatting | bytes 995328 | tf_op jit(solution)/shard_map/jit(_take)/gather | solution.py:136
  186.5 1.3 pad_maximum_fusion
  187.8 0.9 fusion.102
  189.5 0.5 fusion.100
  190.0 3.0 %fusion.106 = (f32[2,6,144]{2,1,0:T(8,128)S(1)}, f32[2,6,144,144]{2,3,1,0:T(8,128)}) fusion(bf16[144,144,2,6]{0,1,3,2:T(8,128)(2,1)S(1)} %copy.61, pred[144,144]{0,1:T(8,128)(4,1)S(1)} %copy.57, pred[2,144,144]{1,2,0:T(8,128)(4,1)} %get-tuple-element.34, bf16[2,1,144,1,6,32]{2,0,5,4,3,1:T(2,128)(2,1)S(1)} %get-tuple-element.20, ...), kind=kOutput, calls=%fused_computation.185 | convolution fusion | flops 17667216 | bytes 1783296 | tf_op jit(solution)/shard_map/sub | solution.py:75
  193.1 1.7 fusion.2
  194.8 0.5 copy.63
  196.7 0.5 fusion.101
  197.2 2.2 %fusion.105 = (f32[2,6,144]{2,1,0:T(8,128)S(1)}, f32[2,6,144,144]{2,3,1,0:T(8,128)}) fusion(bf16[144,144,2,6]{0,1,3,2:T(8,128)(2,1)S(1)} %copy.74, pred[144,144]{0,1:T(8,128)(4,1)S(1)} %copy.57, pred[2,144,144]{1,2,0:T(8,128)(4,1)S(1)} %copy-done.12, bf16[2,1,144,1,6,32]{2,0,5,4,3,1:T(2,128)(2,1)S(1)} %get-tuple-element.23, ...), kind=kOutput, calls=%fused_computation.184 | convolution fusion | flops 17667216 | bytes 1783296 | tf_op jit(solution)/shard_map/sub | solution.py:75
  199.4 1.7 fusion.3
  201.1 0.5 copy.76
  202.5 6.7 %collective-permute-done.6 = bf16[2,6,6,192]{3,0,2,1:T(2,128)(2,1)S(1)} collective-permute-done((bf16[2,6,6,192]{3,0,2,1:T(2,128)(2,1)S(1)}, bf16[2,6,6,192]{3,0,2,1:T(2,128)(2,1)S(1)}, u32[]{:S(2)}, u32[]{:S(2)}) %collective-permute-start.6) | collective-permute-done | bytes 27680 | tf_op jit(solution)/shard_map/ppermute | solution.py:31
  210.0 1.3 fusion.4
  211.3 0.7 copy.79
  (84 shorter events, 5.3 us)
Async XLA Ops:
  0.0 209.9 %copy-start = (bf16[768,192]{0,1:T(8,128)(2,1)S(1)}, bf16[768,192]{0,1:T(8,128)(2,1)}, u32[]{:S(2)}) copy-start(bf16[768,192]{0,1:T(8,128)(2,1)} %param.19) | copy-start | bytes 884740
  0.0 22.7 %copy-start.11 = (bf16[2,1,6,3312]{3,0,2,1:T(2,128)(2,1)S(1)}, bf16[2,1,6,3312]{3,0,2,1:T(2,128)(2,1)}, u32[]{:S(2)}) copy-start(bf16[2,1,6,3312]{3,0,2,1:T(2,128)(2,1)} %param.16) | copy-start | bytes 238468
  0.0 22.6 %collective-permute-start.5 = (bf16[2,1,6,3312]{3,0,2,1:T(2,128)(2,1)}, bf16[2,1,6,3312]{3,0,2,1:T(2,128)(2,1)S(1)}, u32[]{:S(2)}, u32[]{:S(2)}) collective-permute-start(bf16[2,1,6,3312]{3,0,2,1:T(2,128)(2,1)} %param.16), channel_id=1, source_target_pairs={{16,0},{0,16},{17,1},{1,17},{18,2},{2,18},{19,3},{3,19},{20,4},{4,... | collective-permute-start | bytes 238472 | tf_op jit(solution)/shard_map/ppermute | solution.py:31
  6.1 6.4 %collective-permute-start = (bf16[2,6,6,192]{3,2,1,0:T(8,128)(2,1)S(1)}, bf16[2,6,6,192]{3,2,1,0:T(8,128)(2,1)S(1)}, u32[]{:S(2)}, u32[]{:S(2)}) collective-permute-start(bf16[2,6,6,192]{3,2,1,0:T(8,128)(2,1)S(1)} %get-tuple-element.32), channel_id=1, source_target_pairs={{2,0},{4,2},{6,4},{8,6},{10,8},{12,10},{14,12},{0,14},{3,1},{5,3},... | collective-permute-start | bytes 82952 | tf_op jit(solution)/shard_map/ppermute | solution.py:31
  12.6 2.7 %collective-permute-start.1 = (bf16[1,2,3,12,192]{4,3,2,1,0:T(8,128)(2,1)S(1)}, bf16[1,2,3,12,192]{4,3,2,1,0:T(8,128)(2,1)S(1)}, u32[]{:S(2)}, u32[]{:S(2)}) collective-permute-start(bf16[1,2,3,12,192]{4,3,2,1,0:T(8,128)(2,1)S(1)} %bitcast.119), channel_id=1, source_target_pairs={{0,1},{2,3},{4,5},{6,7},{8,9},{10,11},{12,13},{14,15},{16,17},{18,... | collective-permute-start | bytes 82952 | tf_op jit(solution)/shard_map/ppermute | solution.py:22
  13.9 3.1 %collective-permute-start.2 = (bf16[1,2,3,12,192]{4,3,2,1,0:T(8,128)(2,1)S(1)}, bf16[1,2,3,12,192]{4,3,2,1,0:T(8,128)(2,1)S(1)}, u32[]{:S(2)}, u32[]{:S(2)}) collective-permute-start(bf16[1,2,3,12,192]{4,3,2,1,0:T(8,128)(2,1)S(1)} %bitcast.118), channel_id=1, source_target_pairs={{1,0},{3,2},{5,4},{7,6},{9,8},{11,10},{13,12},{15,14},{17,16},{19,... | collective-permute-start | bytes 82952 | tf_op jit(solution)/shard_map/ppermute | solution.py:23
  15.3 7.3 %copy-start.3 = (bf16[2,2,3,12,192]{4,0,3,2,1:T(2,128)(2,1)}, bf16[2,2,3,12,192]{4,0,3,2,1:T(2,128)(2,1)S(1)}, u32[]{:S(2)}) copy-start(bf16[2,2,3,12,192]{4,0,3,2,1:T(2,128)(2,1)S(1)} %copy.50) | copy-start | bytes 165892
  15.4 7.3 %copy-start.5 = (bf16[1,2,3,12,192]{4,0,3,2,1:T(2,128)(2,1)}, bf16[1,2,3,12,192]{4,0,3,2,1:T(2,128)(2,1)S(1)}, u32[]{:S(2)}) copy-start(bf16[1,2,3,12,192]{4,0,3,2,1:T(2,128)(2,1)S(1)} %copy.49) | copy-start | bytes 82948
  17.1 5.6 %copy-start.7 = (bf16[1,2,3,12,192]{4,0,3,2,1:T(2,128)(2,1)}, bf16[1,2,3,12,192]{4,0,3,2,1:T(2,128)(2,1)S(1)}, u32[]{:S(2)}) copy-start(bf16[1,2,3,12,192]{4,0,3,2,1:T(2,128)(2,1)S(1)} %copy.51) | copy-start | bytes 82948
  18.1 168.4 %collective-permute-start.3 = (bf16[4,1,3,12,192]{4,0,3,2,1:T(4,128)(2,1)}, bf16[4,1,3,12,192]{4,0,3,2,1:T(4,128)(2,1)}, u32[]{:S(2)}, u32[]{:S(2)}) collective-permute-start(bf16[4,1,3,12,192]{4,0,3,2,1:T(4,128)(2,1)} %get-tuple-element.28), channel_id=1, source_target_pairs={{0,16},{1,17},{2,18},{3,19},{4,20},{5,21},{6,22},{7,23},{8,24},{9,... | collective-permute-start | bytes 165896 | tf_op jit(solution)/shard_map/ppermute | solution.py:22
  21.1 165.4 %collective-permute-start.4 = (bf16[4,1,3,12,192]{4,0,3,2,1:T(4,128)(2,1)}, bf16[4,1,3,12,192]{4,0,3,2,1:T(4,128)(2,1)}, u32[]{:S(2)}, u32[]{:S(2)}) collective-permute-start(bf16[4,1,3,12,192]{4,0,3,2,1:T(4,128)(2,1)} %get-tuple-element.29), channel_id=1, source_target_pairs={{16,0},{17,1},{18,2},{19,3},{20,4},{21,5},{22,6},{23,7},{24,8},{25... | collective-permute-start | bytes 165896 | tf_op jit(solution)/shard_map/ppermute | solution.py:23
  158.6 27.9 %copy-start.4 = (bf16[2,2,3,12,192]{4,0,3,2,1:T(2,128)(2,1)S(1)}, bf16[2,2,3,12,192]{4,0,3,2,1:T(2,128)(2,1)}, u32[]{:S(2)}) copy-start(bf16[2,2,3,12,192]{4,0,3,2,1:T(2,128)(2,1)} %copy-done.3) | copy-start | bytes 165892
  158.6 27.9 %copy-start.6 = (bf16[1,2,3,12,192]{4,0,3,2,1:T(2,128)(2,1)S(1)}, bf16[1,2,3,12,192]{4,0,3,2,1:T(2,128)(2,1)}, u32[]{:S(2)}) copy-start(bf16[1,2,3,12,192]{4,0,3,2,1:T(2,128)(2,1)} %copy-done.5) | copy-start | bytes 82948
  158.6 27.9 %copy-start.8 = (bf16[1,2,3,12,192]{4,0,3,2,1:T(2,128)(2,1)S(1)}, bf16[1,2,3,12,192]{4,0,3,2,1:T(2,128)(2,1)}, u32[]{:S(2)}) copy-start(bf16[1,2,3,12,192]{4,0,3,2,1:T(2,128)(2,1)} %copy-done.7) | copy-start | bytes 82948
  186.4 2.3 %copy-start.2 = (bf16[192,576]{1,0:T(8,128)(2,1)S(1)}, bf16[192,576]{1,0:T(8,128)(2,1)}, u32[]{:S(2)}) copy-start(bf16[192,576]{1,0:T(8,128)(2,1)} %param.14) | copy-start | bytes 663556
  194.8 1.0 copy-start.9
  195.9 1.3 copy-start.12
  201.1 1.3 copy-start.1
  201.1 8.3 %copy-start.10 = (bf16[192,192]{1,0:T(8,128)(2,1)S(1)}, bf16[192,192]{1,0:T(8,128)(2,1)}, u32[]{:S(2)}) copy-start(bf16[192,192]{1,0:T(8,128)(2,1)} %param.15) | copy-start | bytes 221188
  201.6 8.3 %copy-start.13 = (bf16[192,768]{1,0:T(8,128)(2,1)S(1)}, bf16[192,768]{1,0:T(8,128)(2,1)}, u32[]{:S(2)}) copy-start(bf16[192,768]{1,0:T(8,128)(2,1)} %param.18) | copy-start | bytes 884740
  201.6 8.3 %copy-start.14 = (f32[192]{0:T(256)S(1)}, f32[192]{0:T(256)}, u32[]{:S(2)}) copy-start(f32[192]{0:T(256)} %param.17) | copy-start | bytes 2308
  202.3 7.0 %collective-permute-start.6 = (bf16[2,6,6,192]{3,0,2,1:T(2,128)(2,1)S(1)}, bf16[2,6,6,192]{3,0,2,1:T(2,128)(2,1)S(1)}, u32[]{:S(2)}, u32[]{:S(2)}) collective-permute-start(bf16[2,6,6,192]{3,0,2,1:T(2,128)(2,1)S(1)} %pad_maximum_fusion.4), channel_id=1, source_target_pairs={{14,0},{0,2},{2,4},{4,6},{6,8},{8,10},{10,12},{12,14},{15,1},{1,3}... | collective-permute-start | bytes 82952 | tf_op jit(solution)/shard_map/ppermute | solution.py:31
where the time goes:
time: 213 us; the launch traced here: 212 us
  local copies, waits for them, and re-layouts  170 us (80%)
  starting transfers between devices  14.8 us (7%)
  matrix products  10.8 us (5%)
  waiting for transfers between devices  8.34 us (4%)
  other arithmetic  7.06 us (3%)
    gather x4, local copies, waits for them, and re-layouts, per_device(): bias_terms = jnp.take(lev_tables, table_index, axis=2)  158 us
    ppermute x3, starting transfers between devices, from_behind(): return lax.ppermute(block, axis, route)  7.76 us
    ppermute x3, waiting for transfers between devices, from_behind(): return lax.ppermute(block, axis, route)  6.74 us
    sub x2, matrix products, attend_windows(): weights = jnp.exp(scores - row_max)  5.2 us
    select_n x2, local copies, waits for them, and re-layouts, per_device(): lev_tables = jnp.take(all_tables, lev_type, axis=0)  4.7 us
    ppermute x2, starting transfers between devices, padded(): before = lax.ppermute(last, axis, up)  4.31 us
  transfers between devices with their start and end apart: 7, of which 2 were waited for; matrix products, arithmetic and copies ran while one was open for 80% of the time, Pallas kernels for 0%

commit v1 on v0

v1 whole, which is shorter than its diff:
```python
import functools

import jax
import jax.numpy as jnp
import numpy as np
from jax import lax
from jax.experimental import pallas as pl
from jax.experimental.pallas import tpu as pltpu
from jax.sharding import PartitionSpec as P

HEADS = 6
WLV = 2
WLA = 6
WLO = 12
HALF_LA = WLA // 2
HALF_LO = WLO // 2
OCT = HALF_LA * HALF_LO
PLACES = WLV * WLA * WLO
HALF = PLACES // 2
SPAN = 2 * WLO - 1
CHUNK = WLA * SPAN
ROWS = 8
LANES = 128
AXES = ("lev", "lat", "lon")
BLOCK = WLO * ROWS

norm_eps = 1e-05


def octant_place(lev, lat, lon):
    octant = (lev * 2 + lat // HALF_LA) * 2 + lon // HALF_LO
    return octant * OCT + lat % HALF_LA * HALF_LO + lon % HALF_LO


def spread_matrix():
    spread = np.zeros((PLACES * ROWS, PLACES), np.float32)
    for lev in range(WLV):
        for lat in range(WLA):
            for lon in range(WLO):
                row = ((lev * WLA + lat) * WLO + lon) * ROWS
                spread[row : row + ROWS, octant_place(lev, lat, lon)] = 1
    return spread


def toeplitz_matrix():
    pick = np.zeros((CHUNK, WLO * LANES), np.float32)
    for lon in range(WLO):
        for key_lat in range(WLA):
            for key_lon in range(WLO):
                column = lon * LANES + octant_place(0, key_lat, key_lon)
                pick[key_lat * SPAN + lon - key_lon + WLO - 1, column] = 1
    return pick


def layer_norm(values, scale_gain):
    average = jnp.mean(values, axis=-1, keepdims=True)
    centered = values - average
    variance = jnp.mean(centered * centered, axis=-1, keepdims=True)
    return centered * lax.rsqrt(variance + norm_eps) * scale_gain


def bits_of(octant):
    return (octant >> 2 & 1, octant >> 1 & 1, octant & 1)


def matmul(a, b):
    return jnp.dot(a, b, preferred_element_type=jnp.float32)


def kernel(
    sizes,
    tokens_ref,
    gain1_ref,
    qkv_ref,
    proj_ref,
    table_ref,
    gain2_ref,
    fc1_ref,
    fc2_ref,
    spread_ref,
    gather_ref,
    pick_ref,
    out_ref,
    own,
    send1,
    land1,
    send2,
    land2,
    window,
    table,
    bias,
    scores,
    probs,
    mixed,
    sems,
    rows_out,
):
    where = [lax.axis_index(axis) for axis in AXES]
    features = own.shape[-1]

    def neighbour(octant, sign):
        return {
            axis: lax.rem(at + sign * step + size, size)
            for axis, at, size, step in zip(AXES, where, sizes, bits_of(octant))
        }

    barrier = pltpu.get_barrier_semaphore()
    for octant in range(1, 8):
        for sign in (-1, 1):
            pl.semaphore_signal(
                barrier,
                inc=1,
                device_id=neighbour(octant, sign),
                device_id_type=pl.DeviceIdType.MESH,
            )
    for lev in range(WLV):
        for lat in range(WLA):
            cells = tokens_ref[lev, lat].astype(jnp.float32)
            for side in range(2):
                start = octant_place(lev, lat, side * HALF_LO)
                own[start : start + HALF_LO, :] = cells[side * HALF_LO : (side + 1) * HALF_LO]
    for octant in range(7):
        send1[octant] = own[octant * OCT : (octant + 1) * OCT, :].astype(jnp.bfloat16)
    pl.semaphore_wait(barrier, 14)

    first_copies = []
    for slot in (7, 5, 3, 1, 6, 2, 4):
        copy = pltpu.make_async_remote_copy(
            src_ref=send1.at[7 - slot],
            dst_ref=land1.at[slot],
            send_sem=sems.at[0, slot],
            recv_sem=sems.at[1, slot],
            device_id=neighbour(slot, -1),
            device_id_type=pl.DeviceIdType.MESH,
        )
        copy.start()
        first_copies.append((slot, copy))

    table[...] = jnp.zeros_like(table)
    table[0:HEADS, :] = table_ref[where[0], 0].astype(jnp.float32)
    chunks = jnp.concatenate(
        [table[:, c * CHUNK : (c + 1) * CHUNK] for c in range(WLV * WLV * WLA)], axis=0
    )
    bias[...] = matmul(chunks.astype(jnp.bfloat16), pick_ref[...])

    window[0:OCT, :] = own[7 * OCT : 8 * OCT, :]
    for slot, copy in first_copies:
        copy.wait_recv()
        window[slot * OCT : (slot + 1) * OCT, :] = land1[slot].astype(jnp.float32)

    normed = layer_norm(window[...], gain1_ref[...]).astype(jnp.bfloat16)
    projected = matmul(normed, qkv_ref[...])
    queries = projected[:, :features].astype(jnp.bfloat16)

    def padded_half(values):
        zeros = jnp.zeros((LANES - HALF, features), jnp.float32)
        rows = jnp.concatenate([values[:HALF], zeros, values[HALF:], zeros], axis=0)
        return rows.astype(jnp.bfloat16)

    key_rows = padded_half(projected[:, features : 2 * features])
    value_rows = padded_half(projected[:, 2 * features :])
    row_head = lax.broadcasted_iota(jnp.int32, (PLACES * ROWS, features), 0) % ROWS
    column_head = lax.broadcasted_iota(jnp.int32, (PLACES * ROWS, features), 1) // (
        features // HEADS
    )
    head_mask = row_head == column_head
    spread = jnp.where(head_mask, matmul(spread_ref[...], queries), 0.0).astype(jnp.bfloat16)
    scores[...] = lax.dot_general(
        spread, key_rows, (((1,), (1,)), ((), ())), preferred_element_type=jnp.float32
    )

    lane = lax.broadcasted_iota(jnp.int32, (1, 2 * LANES), 1)
    key_lev = lane // LANES
    key_in = lane % LANES
    key_lat = key_in // (2 * OCT)
    last_lev = where[0] == sizes[0] - 1
    last_lat = where[1] == sizes[1] - 1
    scale = (features // HEADS) ** (-0.5)
    for lev in range(WLV):
        for lat in range(WLA):
            block = (lev * WLA + lat) * BLOCK
            terms = []
            for lon in range(WLO):
                halves = [
                    bias[
                        ((lev * WLV + side) * WLA + lat) * ROWS : ((lev * WLV + side) * WLA + lat)
                        * ROWS
                        + ROWS,
                        lon * LANES : (lon + 1) * LANES,
                    ]
                    for side in range(WLV)
                ]
                terms.append(jnp.concatenate(halves, axis=1))
            keep = key_in < HALF
            keep = keep & ((key_lev == lev) | jnp.logical_not(last_lev))
            keep = keep & ((key_lat == lat // HALF_LA) | jnp.logical_not(last_lat))
            values = scores[block : block + BLOCK, :] * scale + jnp.concatenate(terms, axis=0)
            values = jnp.where(keep, values, -1e30)
            top = jnp.max(values, axis=-1, keepdims=True)
            weights = jnp.exp(values - top)
            total = jnp.sum(weights, axis=-1, keepdims=True)
            probs[block : block + BLOCK, :] = (weights * (1.0 / total)).astype(jnp.bfloat16)

    context = matmul(probs[...], value_rows)
    context = jnp.where(head_mask, context, 0.0).astype(jnp.bfloat16)
    mixed[...] = matmul(gather_ref[...], context)
    for slot in range(1, 8):
        send2[slot] = mixed[slot * OCT : (slot + 1) * OCT, :].astype(jnp.bfloat16)

    second_copies = []
    for slot in (7, 5, 3, 1, 6, 2, 4):
        copy = pltpu.make_async_remote_copy(
            src_ref=send2.at[slot],
            dst_ref=land2.at[7 - slot],
            send_sem=sems.at[2, slot],
            recv_sem=sems.at[3, 7 - slot],
            device_id=neighbour(slot, 1),
            device_id_type=pl.DeviceIdType.MESH,
        )
        copy.start()
        second_copies.append((7 - slot, copy))

    window[7 * OCT : 8 * OCT, :] = mixed[0:OCT, :]
    for octant, copy in second_copies:
        copy.wait_recv()
        window[octant * OCT : (octant + 1) * OCT, :] = land2[octant].astype(jnp.float32)

    first = own[...] + matmul(window[...].astype(jnp.bfloat16), proj_ref[...])
    normed_two = layer_norm(first, gain2_ref[...]).astype(jnp.bfloat16)
    hidden = matmul(normed_two, fc1_ref[...])
    hidden = (0.5 * hidden * (1.0 + lax.erf(hidden * np.float32(0.5**0.5)))).astype(jnp.bfloat16)
    rows_out[...] = first + matmul(hidden, fc2_ref[...])
    for lev in range(WLV):
        for lat in range(WLA):
            for side in range(2):
                start = octant_place(lev, lat, side * HALF_LO)
                out_ref[lev, lat, side * HALF_LO : (side + 1) * HALF_LO, :] = rows_out[
                    start : start + HALF_LO, :
                ].astype(jnp.bfloat16)
    for _, copy in first_copies:
        copy.wait_send()
    for _, copy in second_copies:
        copy.wait_send()


def per_device(
    sizes,
    tokens,
    norm1_gain,
    qkv_weight,
    proj_weight,
    earth_bias,
    norm2_gain,
    fc1_weight,
    fc2_weight,
):
    assert tokens.shape[:3] == (WLV, WLA, WLO)
    features = tokens.shape[-1]
    spread = spread_matrix()
    octants = pltpu.VMEM((8, OCT, features), jnp.bfloat16)
    cells = pltpu.VMEM((PLACES, features), jnp.float32)
    operands = (
        tokens,
        norm1_gain.reshape(1, -1),
        qkv_weight,
        proj_weight,
        earth_bias,
        norm2_gain.reshape(1, -1),
        fc1_weight,
        fc2_weight,
        jnp.asarray(spread, jnp.bfloat16),
        jnp.asarray(spread.T, jnp.bfloat16),
        jnp.asarray(toeplitz_matrix(), jnp.bfloat16),
    )
    return pl.pallas_call(
        functools.partial(kernel, sizes),
        out_shape=jax.ShapeDtypeStruct(tokens.shape, jnp.bfloat16),
        in_specs=[pl.BlockSpec(memory_space=pltpu.VMEM)] * len(operands),
        out_specs=pl.BlockSpec(memory_space=pltpu.VMEM),
        scratch_shapes=[
            cells,
            octants,
            octants,
            octants,
            octants,
            cells,
            pltpu.VMEM((ROWS, earth_bias.shape[-1]), jnp.float32),
            pltpu.VMEM((WLV * WLV * WLA * ROWS, WLO * LANES), jnp.float32),
            pltpu.VMEM((PLACES * ROWS, 2 * LANES), jnp.float32),
            pltpu.VMEM((PLACES * ROWS, 2 * LANES), jnp.bfloat16),
            cells,
            pltpu.SemaphoreType.DMA((4, 8)),
            cells,
        ],
        compiler_params=pltpu.CompilerParams(
            collective_id=0, has_side_effects=True, vmem_limit_bytes=48 * 1024 * 1024
        ),
    )(*operands)


def solution(mesh):
    placed = (
        P("lev", "lat", "lon", None),
        P(),
        P(),
        P(),
        P(None, "lat", None, None),
        P(),
        P(),
        P(),
    )
    return jax.shard_map(
        functools.partial(per_device, tuple(mesh.shape[axis] for axis in AXES)),
        mesh=mesh,
        in_specs=placed,
        out_specs=P("lev", "lat", "lon", None),
        check_vma=False,
    )
```

time: 213 us -> 26.9 us (0.13)
  local copies, waits for them, and re-layouts: 170 us -> 7.55 us
  Pallas kernels: 0 us -> 19 us
  starting transfers between devices: 14.8 us -> 0 us
  matrix products: 10.8 us -> 0 us
  waiting for transfers between devices: 8.34 us -> 0 us
  other arithmetic: 7.06 us -> 0 us
    gather x4 -> x0, local copies, waits for them, and re-layouts: 158 us -> none  [per_device(): bias_terms = jnp.take(lev_tables, table_index, axis=2)]
    pallas_call x0 -> x1, Pallas kernels: none -> 19 us  [per_device(): pl.pallas_call(functools.partial(kernel, sizes), out_shape=jax.ShapeDtype...]
    ppermute x7 -> x0, starting transfers between devices: 14.8 us -> none  [the longest x3 7.76 us: from_behind(): return lax.ppermute(block, axis, route)]
    ppermute x7 -> x0, waiting for transfers between devices: 8.34 us -> none  [the longest x3 6.74 us: from_behind(): return lax.ppermute(block, axis, route)]
    unnamed x31 -> x19, local copies, waits for them, and re-layouts: 0.13 us -> 6.84 us
    dot_general x6 -> x0, matrix products: 5.55 us -> none  [the longest x2 3.42 us: attend_windows(): jnp.einsum('abhqk,abkhd->abqhd', probs, value_rows, preferred_element_typ...]
    sub x2 -> x0, matrix products: 5.2 us -> none  [attend_windows(): weights = jnp.exp(scores - row_max)]
    select_n x2 -> x0, local copies, waits for them, and re-layouts: 4.7 us -> none  [per_device(): lev_tables = jnp.take(all_tables, lev_type, axis=0)]
  transfers between devices with their start and end apart: 7 -> 0, of which waited for: 2 -> 0; matrix products, arithmetic and copies ran while one was open for 80% -> 0% of each run, Pallas kernels for 0% -> 0%
where the time goes in v1:
time: 26.9 us; the launch traced here: 26.7 us
  Pallas kernels  19 us (71%)
  local copies, waits for them, and re-layouts  7.55 us (28%)
    pallas_call x1, Pallas kernels, per_device(): pl.pallas_call(functools.partial(kernel, sizes), out_shape=jax.ShapeDtype...  19 us
    unnamed x19, local copies, waits for them, and re-layouts  6.84 us
    pallas_call x1, local copies, waits for them, and re-layouts, per_device(): pl.pallas_call(functools.partial(kernel, sizes), out_shape=jax.ShapeDtype...  0.71 us

profile of v1, /device:TPU:0, one launch (start us, length us, event | category | flops | bytes accessed | tf_op | source)
XLA Modules:
  0.0 26.7 jit_solution(6463387189087301707)
XLA Ops:
  0.0 0.0 copy-start
  0.0 1.0 %copy.12.tokens_ref = bf16[2,6,12,192]{3,2,1,0:T(8,128)(2,1)S(1)} copy(bf16[2,6,12,192]{3,0,2,1:T(2,128)(2,1)} %param.11) | data formatting | bytes 110592 | tf_op args[0]
  1.0 0.0 copy-start.1
  1.0 1.0 %copy.13.table_ref = bf16[2,1,6,3312]{3,2,1,0:T(8,128)(2,1)S(1)} copy(bf16[2,1,6,3312]{3,0,2,1:T(2,128)(2,1)} %param.15) | data formatting | bytes 158976 | tf_op args[4]
  1.9 0.0 copy-start.6
  1.9 0.0 copy-start.7
  2.0 1.1 %copy.14.fc2_ref = bf16[768,192]{1,0:T(8,128)(2,1)S(1)} copy(bf16[768,192]{0,1:T(8,128)(2,1)} %param.18) | data formatting | bytes 589824 | tf_op args[7]
  3.1 0.0 copy-done
  3.1 0.0 copy-done.1
  3.1 0.0 copy-done.6
  3.1 0.0 copy-done.7
  3.1 0.0 copy-start.2
  3.2 1.0 %copy-done.2 = bf16[144,1152]{1,0:T(8,128)(2,1)S(1)} copy-done((bf16[144,1152]{1,0:T(8,128)(2,1)S(1)}, bf16[144,1152]{1,0:T(8,128)(2,1)}, u32[]{:S(2)}) %copy-start.2) | copy-done | bytes 331800
  4.1 0.0 copy-start.3
  4.1 1.0 %copy-done.3 = bf16[192,768]{1,0:T(8,128)(2,1)S(1)} copy-done((bf16[192,768]{1,0:T(8,128)(2,1)S(1)}, bf16[192,768]{1,0:T(8,128)(2,1)}, u32[]{:S(2)}) %copy-start.3) | copy-done | bytes 294936
  5.1 0.0 copy-start.4
  5.1 0.9 %copy-done.4 = bf16[192,576]{1,0:T(8,128)(2,1)S(1)} copy-done((bf16[192,576]{1,0:T(8,128)(2,1)S(1)}, bf16[192,576]{1,0:T(8,128)(2,1)}, u32[]{:S(2)}) %copy-start.4) | copy-done | bytes 221208
  6.0 0.0 copy-start.5
  6.0 0.9 %copy-done.5 = bf16[192,192]{1,0:T(8,128)(2,1)S(1)} copy-done((bf16[192,192]{1,0:T(8,128)(2,1)S(1)}, bf16[192,192]{1,0:T(8,128)(2,1)}, u32[]{:S(2)}) %copy-start.5) | copy-done | bytes 73752
  6.9 19.0 %shard_map.109 = bf16[2,6,12,192]{3,2,1,0:T(8,128)(2,1)S(1)} custom-call(bf16[2,6,12,192]{3,2,1,0:T(8,128)(2,1)S(1)} %copy.12.tokens_ref, f32[1,192]{1,0:T(1,128)S(1)} %bitcast.2, bf16[192,576]{1,0:T(8,128)(2,1)S(1)} %copy-done.4, bf16[192,192]{1,0:T(8,128)(2,1)S(1)} %copy-done.5, bf16[2,1,6,3312]{3,2,1,0:T(8,128)(2,1)S(1)} %copy.13.table_ref, ...), custom_call_target="tpu_custom_call" | custom-call | tf_op jit(solution)/shard_map/pallas_call | solution.py:275
  25.9 0.7 %copy.15 = bf16[2,6,12,192]{3,0,2,1:T(2,128)(2,1)} copy(bf16[2,6,12,192]{3,2,1,0:T(8,128)(2,1)S(1)} %shard_map.109) | data formatting | bytes 110592 | tf_op jit(solution)/shard_map/pallas_call | solution.py:275
Async XLA Ops:
  0.0 3.1 %copy-start = (bf16[1152,144]{1,0:T(8,128)(2,1)S(1)}, bf16[1152,144]{1,0:T(8,128)(2,1)}, u32[]{:S(2)}) copy-start(bf16[1152,144]{1,0:T(8,128)(2,1)} %constant.6.clone.spread_ref) | copy-start | bytes 995332
  1.0 2.1 %copy-start.1 = (bf16[138,1536]{1,0:T(8,128)(2,1)S(1)}, bf16[138,1536]{1,0:T(8,128)(2,1)}, u32[]{:S(2)}) copy-start(bf16[138,1536]{1,0:T(8,128)(2,1)} %constant.8.clone.pick_ref) | copy-start | bytes 1271812
  1.9 1.2 %copy-start.6 = (f32[192]{0:T(256)S(1)}, f32[192]{0:T(256)}, u32[]{:S(2)}) copy-start(f32[192]{0:T(256)} %param.12) | copy-start | bytes 2308
  1.9 1.2 %copy-start.7 = (f32[192]{0:T(256)S(1)}, f32[192]{0:T(256)}, u32[]{:S(2)}) copy-start(f32[192]{0:T(256)} %param.16) | copy-start | bytes 2308
  3.1 1.0 %copy-start.2 = (bf16[144,1152]{1,0:T(8,128)(2,1)S(1)}, bf16[144,1152]{1,0:T(8,128)(2,1)}, u32[]{:S(2)}) copy-start(bf16[144,1152]{1,0:T(8,128)(2,1)} %constant.7.clone.gather_ref) | copy-start | bytes 995332
  4.1 1.0 %copy-start.3 = (bf16[192,768]{1,0:T(8,128)(2,1)S(1)}, bf16[192,768]{1,0:T(8,128)(2,1)}, u32[]{:S(2)}) copy-start(bf16[192,768]{1,0:T(8,128)(2,1)} %fc1_ref.1) | copy-start | bytes 884740
  5.1 0.9 %copy-start.4 = (bf16[192,576]{1,0:T(8,128)(2,1)S(1)}, bf16[192,576]{1,0:T(8,128)(2,1)}, u32[]{:S(2)}) copy-start(bf16[192,576]{1,0:T(8,128)(2,1)} %qkv_ref.1) | copy-start | bytes 663556
  6.0 0.9 %copy-start.5 = (bf16[192,192]{1,0:T(8,128)(2,1)S(1)}, bf16[192,192]{1,0:T(8,128)(2,1)}, u32[]{:S(2)}) copy-start(bf16[192,192]{1,0:T(8,128)(2,1)} %proj_ref.1) | copy-start | bytes 221188

commit v2 on v1

--- a/solution.py
+++ b/solution.py
@@ -23,6 +23,7 @@
 LANES = 128
 AXES = ("lev", "lat", "lon")
 BLOCK = WLO * ROWS
+OPERANDS = 11
 
 norm_eps = 1e-05
 
@@ -67,85 +68,134 @@
     return jnp.dot(a, b, preferred_element_type=jnp.float32)
 
 
-def kernel(
-    sizes,
-    tokens_ref,
-    gain1_ref,
-    qkv_ref,
-    proj_ref,
-    table_ref,
-    gain2_ref,
-    fc1_ref,
-    fc2_ref,
-    spread_ref,
-    gather_ref,
-    pick_ref,
-    out_ref,
-    own,
-    send1,
-    land1,
-    send2,
-    land2,
-    window,
-    table,
-    bias,
-    scores,
-    probs,
-    mixed,
-    sems,
-    rows_out,
-):
+def kernel(sizes, *refs):
+    operands, out_ref, held = refs[:OPERANDS], refs[OPERANDS], refs[OPERANDS + 1 : -14]
+    (
+        own,
+        send1,
+        land1,
+        send2,
+        land2,
+        window,
+        table,
+        bias,
+        scores,
+        probs,
+        mixed,
+        sems,
+        rows_out,
+        load_sems,
+    ) = refs[-14:]
+    loads = [
+        pltpu.make_async_copy(source, place, load_sems.at[i])
+        for i, (source, place) in enumerate(zip(operands, held))
+    ]
+    for load in loads:
+        load.start()
+    (
+        tokens_ref,
+        table_ref,
+        pick_ref,
+        gain1_ref,
+        qkv_ref,
+        spread_ref,
+        gather_ref,
+        proj_ref,
+        gain2_ref,
+        fc1_ref,
+        fc2_ref,
+    ) = held
     where = [lax.axis_index(axis) for axis in AXES]
     features = own.shape[-1]
-
-    def neighbour(octant, sign):
-        return {
+    count = sizes[2]
+    middle = count // 2 - 1
+    mine = where[2]
+    my_window = jnp.where(mine < middle, mine, jnp.where(mine == middle, count - 1, mine - 1))
+    keeps_slot = {0: mine < middle, 1: mine > middle}
+
+    def worker(lon_window):
+        return jnp.where(
+            lon_window < middle,
+            lon_window,
+            jnp.where(lon_window == count - 1, middle, lon_window + 1),
+        )
+
+    def device(slot, sign, lon):
+        place = {
             axis: lax.rem(at + sign * step + size, size)
-            for axis, at, size, step in zip(AXES, where, sizes, bits_of(octant))
+            for axis, at, size, step in zip(AXES[:2], where, sizes, bits_of(slot))
         }
+        place["lon"] = lon
+        return place
+
+    def window_device(slot):
+        return device(slot, -1, worker(lax.rem(mine - bits_of(slot)[2] + count, count)))
+
+    def cell_device(slot):
+        return device(slot, 1, lax.rem(my_window + bits_of(slot)[2], count))
+
+    def unless_mine(slot, action, otherwise=None):
+        if slot not in keeps_slot:
+            action()
+            return
+        pl.when(jnp.logical_not(keeps_slot[slot]))(action)
+        if otherwise is not None:
+            pl.when(keeps_slot[slot])(otherwise)
 
     barrier = pltpu.get_barrier_semaphore()
-    for octant in range(1, 8):
-        for sign in (-1, 1):
-            pl.semaphore_signal(
-                barrier,
-                inc=1,
-                device_id=neighbour(octant, sign),
-                device_id_type=pl.DeviceIdType.MESH,
-            )
-    for lev in range(WLV):
-        for lat in range(WLA):
-            cells = tokens_ref[lev, lat].astype(jnp.float32)
-            for side in range(2):
-                start = octant_place(lev, lat, side * HALF_LO)
-                own[start : start + HALF_LO, :] = cells[side * HALF_LO : (side + 1) * HALF_LO]
-    for octant in range(7):
+    for slot in range(8):
+
+        def greet(slot=slot):
+            for there in (window_device(slot), cell_device(slot)):
+                pl.semaphore_signal(
+                    barrier, inc=1, device_id=there, device_id_type=pl.DeviceIdType.MESH
+                )
+
+        unless_mine(slot, greet)
+    loads[0].wait()
+    for lat in range(WLA):
+        for lon in range(WLO):
+            cell = tokens_ref[lat, lon].astype(jnp.float32)
+            for lev in range(WLV):
+                place = octant_place(lev, lat, lon)
+                own[place : place + 1, :] = cell[lev : lev + 1]
+    for octant in range(8):
         send1[octant] = own[octant * OCT : (octant + 1) * OCT, :].astype(jnp.bfloat16)
-    pl.semaphore_wait(barrier, 14)
-
+    pl.semaphore_wait(barrier, jnp.where(mine == middle, 16, 14))
+
+    order = (7, 5, 3, 1, 6, 4, 2, 0)
     first_copies = []
-    for slot in (7, 5, 3, 1, 6, 2, 4):
+    for slot in order:
         copy = pltpu.make_async_remote_copy(
             src_ref=send1.at[7 - slot],
             dst_ref=land1.at[slot],
             send_sem=sems.at[0, slot],
             recv_sem=sems.at[1, slot],
-            device_id=neighbour(slot, -1),
+            device_id=window_device(slot),
             device_id_type=pl.DeviceIdType.MESH,
         )
-        copy.start()
+
+        def keep(slot=slot):
+            land1[slot] = send1[7 - slot]
+
+        unless_mine(slot, copy.start, keep)
         first_copies.append((slot, copy))
 
+    loads[1].wait()
+    loads[2].wait()
     table[...] = jnp.zeros_like(table)
-    table[0:HEADS, :] = table_ref[where[0], 0].astype(jnp.float32)
+    for head in range(HEADS):
+        pair = table_ref[0, head].astype(jnp.float32)
+        table[head : head + 1, :] = jnp.where(where[0] == 0, pair[0:1], pair[1:2])
     chunks = jnp.concatenate(
         [table[:, c * CHUNK : (c + 1) * CHUNK] for c in range(WLV * WLV * WLA)], axis=0
     )
     bias[...] = matmul(chunks.astype(jnp.bfloat16), pick_ref[...])
 
-    window[0:OCT, :] = own[7 * OCT : 8 * OCT, :]
+    for load in loads[3:]:
+        load.wait()
     for slot, copy in first_copies:
-        copy.wait_recv()
+        unless_mine(slot, copy.wait_recv)
         window[slot * OCT : (slot + 1) * OCT, :] = land1[slot].astype(jnp.float32)
 
     normed = layer_norm(window[...], gain1_ref[...]).astype(jnp.bfloat16)
@@ -204,43 +254,46 @@
     context = matmul(probs[...], value_rows)
     context = jnp.where(head_mask, context, 0.0).astype(jnp.bfloat16)
     mixed[...] = matmul(gather_ref[...], context)
-    for slot in range(1, 8):
+    for slot in range(8):
         send2[slot] = mixed[slot * OCT : (slot + 1) * OCT, :].astype(jnp.bfloat16)
 
     second_copies = []
-    for slot in (7, 5, 3, 1, 6, 2, 4):
+    for slot in order:
         copy = pltpu.make_async_remote_copy(
             src_ref=send2.at[slot],
             dst_ref=land2.at[7 - slot],
             send_sem=sems.at[2, slot],
-            recv_sem=sems.at[3, 7 - slot],
-            device_id=neighbour(slot, 1),
+            recv_sem=sems.at[3, slot],
+            device_id=cell_device(slot),
             device_id_type=pl.DeviceIdType.MESH,
         )
-        copy.start()
-        second_copies.append((7 - slot, copy))
-
-    window[7 * OCT : 8 * OCT, :] = mixed[0:OCT, :]
-    for octant, copy in second_copies:
-        copy.wait_recv()
+
+        def keep(slot=slot):
+            land2[7 - slot] = send2[slot]
+
+        unless_mine(slot, copy.start, keep)
+        second_copies.append((slot, copy))
+
+    for slot, copy in second_copies:
+        unless_mine(slot, copy.wait_recv)
+        octant = 7 - slot
         window[octant * OCT : (octant + 1) * OCT, :] = land2[octant].astype(jnp.float32)
 
     first = own[...] + matmul(window[...].astype(jnp.bfloat16), proj_ref[...])
     normed_two = layer_norm(first, gain2_ref[...]).astype(jnp.bfloat16)
     hidden = matmul(normed_two, fc1_ref[...])
     hidden = (0.5 * hidden * (1.0 + lax.erf(hidden * np.float32(0.5**0.5)))).astype(jnp.bfloat16)
-    rows_out[...] = first + matmul(hidden, fc2_ref[...])
-    for lev in range(WLV):
-        for lat in range(WLA):
-            for side in range(2):
-                start = octant_place(lev, lat, side * HALF_LO)
-                out_ref[lev, lat, side * HALF_LO : (side + 1) * HALF_LO, :] = rows_out[
-                    start : start + HALF_LO, :
-                ].astype(jnp.bfloat16)
-    for _, copy in first_copies:
-        copy.wait_send()
-    for _, copy in second_copies:
-        copy.wait_send()
+    rows_out[...] = first + lax.dot_general(
+        hidden, fc2_ref[...], (((1,), (1,)), ((), ())), preferred_element_type=jnp.float32
+    )
+    for lat in range(WLA):
+        for lon in range(WLO):
+            places = [octant_place(lev, lat, lon) for lev in range(WLV)]
+            out_ref[lat, lon] = jnp.concatenate(
+                [rows_out[place : place + 1, :] for place in places], axis=0
+            ).astype(jnp.bfloat16)
+    for slot, copy in first_copies + second_copies:
+        unless_mine(slot, copy.wait_send)
 
 
 def per_device(
@@ -260,24 +313,26 @@
     octants = pltpu.VMEM((8, OCT, features), jnp.bfloat16)
     cells = pltpu.VMEM((PLACES, features), jnp.float32)
     operands = (
-        tokens,
+        tokens.transpose(1, 2, 0, 3),
+        earth_bias.transpose(1, 2, 0, 3),
+        jnp.asarray(toeplitz_matrix(), jnp.bfloat16),
         norm1_gain.reshape(1, -1),
         qkv_weight,
+        jnp.asarray(spread, jnp.bfloat16),
+        jnp.asarray(spread.T, jnp.bfloat16),
         proj_weight,
-        earth_bias,
         norm2_gain.reshape(1, -1),
         fc1_weight,
-        fc2_weight,
-        jnp.asarray(spread, jnp.bfloat16),
-        jnp.asarray(spread.T, jnp.bfloat16),
-        jnp.asarray(toeplitz_matrix(), jnp.bfloat16),
-    )
-    return pl.pallas_call(
+        fc2_weight.T,
+    )
+    assert len(operands) == OPERANDS
+    blended = pl.pallas_call(
         functools.partial(kernel, sizes),
-        out_shape=jax.ShapeDtypeStruct(tokens.shape, jnp.bfloat16),
-        in_specs=[pl.BlockSpec(memory_space=pltpu.VMEM)] * len(operands),
+        out_shape=jax.ShapeDtypeStruct(operands[0].shape, jnp.bfloat16),
+        in_specs=[pl.BlockSpec(memory_space=pltpu.HBM)] * OPERANDS,
         out_specs=pl.BlockSpec(memory_space=pltpu.VMEM),
         scratch_shapes=[
+            *[pltpu.VMEM(operand.shape, operand.dtype) for operand in operands],
             cells,
             octants,
             octants,
@@ -291,11 +346,13 @@
             cells,
             pltpu.SemaphoreType.DMA((4, 8)),
             cells,
+            pltpu.SemaphoreType.DMA((OPERANDS,)),
         ],
         compiler_params=pltpu.CompilerParams(
-            collective_id=0, has_side_effects=True, vmem_limit_bytes=48 * 1024 * 1024
+            collective_id=0, has_side_effects=True, vmem_limit_bytes=67_043_328
         ),
     )(*operands)
+    return blended.transpose(2, 0, 1, 3)
 
 
 def solution(mesh):

time: 26.9 us -> 18.2 us (0.68)
  local copies, waits for them, and re-layouts: 7.55 us -> 1.57 us
  Pallas kernels: 19 us -> 16.5 us
    unnamed x19 -> x1, local copies, waits for them, and re-layouts: 6.84 us -> 1.57 us
    pallas_call x1, Pallas kernels: 19 us -> 16.5 us  [per_device(): pl.pallas_call(functools.partial(kernel, sizes), out_shape=jax.ShapeDtype...]
    pallas_call x1 -> x0, local copies, waits for them, and re-layouts: 0.71 us -> none  [per_device(): pl.pallas_call(functools.partial(kernel, sizes), out_shape=jax.ShapeDtype...]
where the time goes in v2:
time: 18.2 us; the launch traced here: 18 us
  Pallas kernels  16.5 us (91%)
  local copies, waits for them, and re-layouts  1.57 us (9%)
    pallas_call x1, Pallas kernels, per_device(): pl.pallas_call(functools.partial(kernel, sizes), out_shape=jax.ShapeDtype...  16.5 us
    unnamed x1, local copies, waits for them, and re-layouts  1.57 us

profile of v2, /device:TPU:0, one launch (start us, length us, event | category | flops | bytes accessed | tf_op | source)
XLA Modules:
  0.0 18.0 jit_solution(13418506452159681477)
XLA Ops:
  0.0 16.5 %shard_map.109 = bf16[6,12,2,192]{3,2,1,0:T(2,128)(2,1)} custom-call(bf16[6,12,2,192]{3,2,1,0:T(2,128)(2,1)} %bitcast.9, bf16[1,6,2,3312]{3,2,1,0:T(2,128)(2,1)} %bitcast.8, bf16[138,1536]{1,0:T(8,128)(2,1)} %constant.6.clone.refs_2_, f32[1,192]{1,0:T(1,128)} %bitcast.10, bf16[192,576]{1,0:T(8,128)(2,1)} %refs_4_.1, ...), custom_call_target="tpu_custom_call" | custom-call | tf_op jit(solution)/shard_map/pallas_call | solution.py:329
  16.5 1.6 %copy.13 = bf16[2,6,12,192]{3,0,2,1:T(2,128)(2,1)} copy(bf16[2,6,12,192]{3,0,2,1:T(2,128)(2,1)} %bitcast.7) | data formatting | bytes 110592

commit v3 on v2

--- a/solution.py
+++ b/solution.py
@@ -58,6 +58,16 @@
     centered = values - average
     variance = jnp.mean(centered * centered, axis=-1, keepdims=True)
     return centered * lax.rsqrt(variance + norm_eps) * scale_gain
+
+
+def window_workers(count):
+    middle = count // 2 - 1
+    if count % 4:
+        low = list(range(middle))
+        return low + list(range(middle + 1, count)) + [middle]
+    low = [w ^ 1 for w in range(middle - 1)] + [middle - 1]
+    high = [w + 2 if w % 2 else w for w in range(middle, count - 1)]
+    return low + high + [middle]
 
 
 def bits_of(octant):
@@ -108,17 +118,21 @@
     where = [lax.axis_index(axis) for axis in AXES]
     features = own.shape[-1]
     count = sizes[2]
-    middle = count // 2 - 1
     mine = where[2]
-    my_window = jnp.where(mine < middle, mine, jnp.where(mine == middle, count - 1, mine - 1))
-    keeps_slot = {0: mine < middle, 1: mine > middle}
+    workers = window_workers(count)
+
+    def entry(values, index):
+        found = jnp.int32(values[0])
+        for i, value in enumerate(values[1:], 1):
+            found = jnp.where(index == i, value, found)
+        return found
+
+    my_window = entry([workers.index(i) for i in range(count)], mine)
+    keeps_slot = {0: my_window == mine, 1: lax.rem(my_window + 1, count) == mine}
+    keeps_none = jnp.logical_not(keeps_slot[0] | keeps_slot[1])
 
     def worker(lon_window):
-        return jnp.where(
-            lon_window < middle,
-            lon_window,
-            jnp.where(lon_window == count - 1, middle, lon_window + 1),
-        )
+        return entry(workers, lon_window)
 
     def device(slot, sign, lon):
         place = {
@@ -159,9 +173,11 @@
             for lev in range(WLV):
                 place = octant_place(lev, lat, lon)
                 own[place : place + 1, :] = cell[lev : lev + 1]
+    loads[3].wait()
+    window[...] = layer_norm(own[...], gain1_ref[...])
     for octant in range(8):
-        send1[octant] = own[octant * OCT : (octant + 1) * OCT, :].astype(jnp.bfloat16)
-    pl.semaphore_wait(barrier, jnp.where(mine == middle, 16, 14))
+        send1[octant] = window[octant * OCT : (octant + 1) * OCT, :].astype(jnp.bfloat16)
+    pl.semaphore_wait(barrier, jnp.where(keeps_none, 16, 14))
 
     order = (7, 5, 3, 1, 6, 4, 2, 0)
     first_copies = []
@@ -192,13 +208,13 @@
     )
     bias[...] = matmul(chunks.astype(jnp.bfloat16), pick_ref[...])
 
-    for load in loads[3:]:
+    for load in loads[4:]:
         load.wait()
     for slot, copy in first_copies:
         unless_mine(slot, copy.wait_recv)
         window[slot * OCT : (slot + 1) * OCT, :] = land1[slot].astype(jnp.float32)
 
-    normed = layer_norm(window[...], gain1_ref[...]).astype(jnp.bfloat16)
+    normed = window[...].astype(jnp.bfloat16)
     projected = matmul(normed, qkv_ref[...])
     queries = projected[:, :features].astype(jnp.bfloat16)
 
@@ -209,12 +225,15 @@
 
     key_rows = padded_half(projected[:, features : 2 * features])
     value_rows = padded_half(projected[:, 2 * features :])
-    row_head = lax.broadcasted_iota(jnp.int32, (PLACES * ROWS, features), 0) % ROWS
-    column_head = lax.broadcasted_iota(jnp.int32, (PLACES * ROWS, features), 1) // (
-        features // HEADS
-    )
-    head_mask = row_head == column_head
-    spread = jnp.where(head_mask, matmul(spread_ref[...], queries), 0.0).astype(jnp.bfloat16)
+    row_head = lax.broadcasted_iota(jnp.int32, (ROWS, features), 0)
+    column_head = lax.broadcasted_iota(jnp.int32, (ROWS, features), 1) // (features // HEADS)
+    own_head = (row_head == column_head)[None]
+
+    def of_own_head(values):
+        tiles = values.reshape(PLACES, ROWS, features)
+        return jnp.where(own_head, tiles, 0.0).reshape(values.shape).astype(jnp.bfloat16)
+
+    spread = of_own_head(matmul(spread_ref[...], queries))
     scores[...] = lax.dot_general(
         spread, key_rows, (((1,), (1,)), ((), ())), preferred_element_type=jnp.float32
     )
@@ -251,8 +270,7 @@
             total = jnp.sum(weights, axis=-1, keepdims=True)
             probs[block : block + BLOCK, :] = (weights * (1.0 / total)).astype(jnp.bfloat16)
 
-    context = matmul(probs[...], value_rows)
-    context = jnp.where(head_mask, context, 0.0).astype(jnp.bfloat16)
+    context = of_own_head(matmul(probs[...], value_rows))
     mixed[...] = matmul(gather_ref[...], context)
     for slot in range(8):
         send2[slot] = mixed[slot * OCT : (slot + 1) * OCT, :].astype(jnp.bfloat16)

time: 18.2 us -> 18 us (0.989)
  Pallas kernels: 16.5 us -> 16.3 us
where the time goes in v3:
time: 18 us; the launch traced here: 17.9 us
  Pallas kernels  16.3 us (91%)
  local copies, waits for them, and re-layouts  1.57 us (9%)
    pallas_call x1, Pallas kernels, per_device(): pl.pallas_call(functools.partial(kernel, sizes), out_shape=jax.ShapeDtype...  16.3 us
    unnamed x1, local copies, waits for them, and re-layouts  1.57 us

profile of v3, /device:TPU:0, one launch (start us, length us, event | category | flops | bytes accessed | tf_op | source)
XLA Modules:
  0.0 17.9 jit_solution(12156046000980593555)
XLA Ops:
  0.0 16.3 %shard_map.109 = bf16[6,12,2,192]{3,2,1,0:T(2,128)(2,1)} custom-call(bf16[6,12,2,192]{3,2,1,0:T(2,128)(2,1)} %bitcast.9, bf16[1,6,2,3312]{3,2,1,0:T(2,128)(2,1)} %bitcast.8, bf16[138,1536]{1,0:T(8,128)(2,1)} %constant.6.clone.refs_2_, f32[1,192]{1,0:T(1,128)} %bitcast.10, bf16[192,576]{1,0:T(8,128)(2,1)} %refs_4_.1, ...), custom_call_target="tpu_custom_call" | custom-call | tf_op jit(solution)/shard_map/pallas_call | solution.py:347
  16.3 1.6 %copy.13 = bf16[2,6,12,192]{3,0,2,1:T(2,128)(2,1)} copy(bf16[2,6,12,192]{3,0,2,1:T(2,128)(2,1)} %bitcast.7) | data formatting | bytes 110592

commit v4 on v3

--- a/solution.py
+++ b/solution.py
@@ -367,9 +367,9 @@
             pltpu.SemaphoreType.DMA((OPERANDS,)),
         ],
         compiler_params=pltpu.CompilerParams(
-            collective_id=0, has_side_effects=True, vmem_limit_bytes=67_043_328
+            collective_id=0, has_side_effects=True, vmem_limit_bytes=48 * 1024 * 1024
         ),
-    )(*operands)
+    )(*[pltpu.with_memory_space_constraint(x, pltpu.HBM) for x in operands])
     return blended.transpose(2, 0, 1, 3)
 
 

time: 18 us -> 16.5 us (0.917)
  local copies, waits for them, and re-layouts: 1.57 us -> 0.64 us
  Pallas kernels: 16.3 us -> 15.7 us
    unnamed x1, local copies, waits for them, and re-layouts: 1.57 us -> 0.64 us
    pallas_call x1, Pallas kernels: 16.3 us -> 15.7 us  [per_device(): pl.pallas_call(functools.partial(kernel, sizes), out_shape=jax.ShapeDtype...]
where the time goes in v4:
time: 16.5 us; the launch traced here: 16.3 us
  Pallas kernels  15.7 us (95%)
  local copies, waits for them, and re-layouts  0.64 us (4%)
    pallas_call x1, Pallas kernels, per_device(): pl.pallas_call(functools.partial(kernel, sizes), out_shape=jax.ShapeDtype...  15.7 us
    unnamed x1, local copies, waits for them, and re-layouts  0.64 us

profile of v4, /device:TPU:0, one launch (start us, length us, event | category | flops | bytes accessed | tf_op | source)
XLA Modules:
  0.0 16.3 jit_solution(7785959172849280151)
XLA Ops:
  0.0 15.7 %shard_map.109 = bf16[6,12,2,192]{3,2,1,0:T(2,128)(2,1)S(1)} custom-call(bf16[6,12,2,192]{3,2,1,0:T(2,128)(2,1)} %bitcast.9, bf16[1,6,2,3312]{3,2,1,0:T(2,128)(2,1)} %bitcast.8, bf16[138,1536]{1,0:T(8,128)(2,1)} %constant.6.clone.refs_2_, f32[1,192]{1,0:T(1,128)} %bitcast.10, bf16[192,576]{1,0:T(8,128)(2,1)} %refs_4_.1, ...), custom_call_target="tpu_custom_call" | custom-call | tf_op jit(solution)/shard_map/pallas_call | solution.py:347
  15.7 0.6 %copy.13 = bf16[2,6,12,192]{3,0,2,1:T(2,128)(2,1)} copy(bf16[2,6,12,192]{3,0,2,1:T(2,128)(2,1)S(1)} %bitcast.6) | data formatting | bytes 110592
